TPU v7x, 512 devices: a whole 4x4x16 slice. The times are simulated.
512 devices in a mesh: tm: 128 (over x, z, core), head: 4 (over y).
Axes of the slice: x: 4, y: 4, z: 16, core: 2. Of those that a mesh axis runs over, the one named last changes fastest.
Arguments:
- latent: bfloat16 [65536, 1024], P('tm', 'head'), may hold values from -6 to 6
- timestep: int32 [1], replicated, may hold values from 0 to 999
- in_gain: float32 [1024], replicated, may hold values from 0.1 to 1.9
- w_x: bfloat16 [1024, 2048], P(None, 'head'), may hold values from -0.1875 to 0.1875
- w_z: bfloat16 [1024, 2048], P(None, 'head'), may hold values from -0.1875 to 0.1875
- w_bc: bfloat16 [1024, 256], replicated, may hold values from -0.1875 to 0.1875
- w_dt: bfloat16 [1024, 32], P(None, 'head'), may hold values from -0.1875 to 0.1875
- conv_x: float32 [4, 2048], P(None, 'head'), may hold values from -3 to 3
- conv_bc: float32 [4, 256], replicated, may hold values from -3 to 3
- dt_bias: float32 [32], P('head'), may hold values from -1 to 0.5
- a_log: float32 [32], P('head'), may hold values from -13 to -1, as said below
- d_skip: float32 [32], P('head'), may hold values from 4 to 64
- norm_gain: float32 [2048], P('head'), may hold values from 0.1 to 1.9
- w_out: bfloat16 [2048, 1024], P('head'), may hold values from -0.125 to 0.125
- w_mix: bfloat16 [1024, 1024], P(None, 'head'), may hold values from -0.1875 to 0.1875
Outputs:
- denoised: bfloat16 [65536, 1024], P('tm', 'head')
Inputs may be any that keep to these rules, and one draw needn't show every extreme that they name: `a_log`: the logarithm of each head's decay rate.
All inputs are finite; a program needn't handle non-finite values.
Results may differ from a plain program's by a relative error of at most 0.012.
Values may be sent and summed in bfloat16 or wider, within the bound.
A program may use at most 128 MiB of HBM per device.

v0:
```python
import math
import jax
import jax.numpy as jnp
from jax import lax
from jax.sharding import PartitionSpec as P

BLOCK = 256


def from_behind(block, axis, distance):
    devices = range(lax.axis_size(axis))
    route = [(i - distance, i) for i in devices if i - distance in devices]
    return lax.ppermute(block, axis, route)


def prefix(part, axis, combine, identity):
    place = lax.axis_index(axis)
    gathered = jax.tree.map(lambda a: lax.all_gather(a, axis), part)
    state = jax.tree.map(lambda a, e: jnp.zeros_like(a) + jnp.asarray(e, a.dtype), part, identity)

    def one(hop, state):
        return combine(
            state, jax.tree.map(lambda a: lax.dynamic_index_in_dim(a, hop, 0, False), gathered)
        )

    return lax.fori_loop(0, place, one, state)


def sinusoid(timestep, width):
    half = width // 2
    freq = jnp.exp(-math.log(10000.0) * jnp.arange(half, dtype=jnp.float32) / half)
    angle = timestep.astype(jnp.float32)[0] * freq
    return jnp.concatenate([jnp.sin(angle), jnp.cos(angle)])


def causal_conv(rows, rim, kernel):
    padded = jnp.concatenate([rim, rows], axis=0)
    count = rows.shape[0]
    total = jnp.zeros(rows.shape, jnp.float32)
    for k in range(kernel.shape[0]):
        total = total + padded[k : k + count].astype(jnp.float32) * kernel[k]
    return jax.nn.silu(total).astype(jnp.bfloat16)


def block_terms(xa, bmat, cmat, dt, la):
    steps = xa.shape[0]
    cum = jnp.cumsum(la, axis=0)
    scores = jnp.dot(cmat, bmat.T, preferred_element_type=jnp.float32)
    rowid = lax.broadcasted_iota(jnp.int32, (steps, steps), 0)
    colid = lax.broadcasted_iota(jnp.int32, (steps, steps), 1)
    causal = rowid >= colid
    cumt = cum.T
    seg = cumt[:, :, None] - cumt[:, None, :]
    decay = jnp.exp(jnp.where(causal[None], seg, -jnp.inf))
    mixw = (scores[None] * decay * dt.T[:, None, :]).astype(jnp.bfloat16)
    ydiag = jnp.einsum("hij,jhp->ihp", mixw, xa, preferred_element_type=jnp.float32)
    tail = jnp.exp(cum[-1][None, :] - cum) * dt
    weighted = (bmat.astype(jnp.float32)[:, None, :] * tail[:, :, None]).astype(jnp.bfloat16)
    state = jnp.einsum("jhn,jhp->hnp", weighted, xa, preferred_element_type=jnp.float32)
    total = jnp.exp(cum[-1])
    return (ydiag, state, total, cum)


def block_output(ydiag, cum, cmat, hin, xa, d_skip):
    yoff = jnp.einsum(
        "in,hnp->ihp", cmat, hin.astype(jnp.bfloat16), preferred_element_type=jnp.float32
    )
    yoff = yoff * jnp.exp(cum)[:, :, None]
    return ydiag + yoff + d_skip[None, :, None] * xa.astype(jnp.float32)


def combine_states(earlier, later):
    return (earlier[0] * later[0], earlier[1] * later[0][:, None, None] + later[1])


def shards(
    latent,
    timestep,
    in_gain,
    w_x,
    w_z,
    w_bc,
    w_dt,
    conv_x,
    conv_bc,
    dt_bias,
    a_log,
    d_skip,
    norm_gain,
    w_out,
    w_mix,
):
    whole = lax.all_gather(latent, "head", axis=1, tiled=True)
    u = whole.astype(jnp.float32) + sinusoid(timestep, whole.shape[1])[None, :]
    normed = (u * lax.rsqrt(jnp.mean(u * u, axis=1, keepdims=True) + 1e-05) * in_gain).astype(
        jnp.bfloat16
    )
    xs = jnp.dot(normed, w_x, preferred_element_type=jnp.float32).astype(jnp.bfloat16)
    gate = jnp.dot(normed, w_z, preferred_element_type=jnp.float32).astype(jnp.bfloat16)
    bc = jnp.dot(normed, w_bc, preferred_element_type=jnp.float32).astype(jnp.bfloat16)
    dt_raw = jnp.dot(normed, w_dt, preferred_element_type=jnp.float32)
    width = conv_x.shape[0] - 1
    steps_dev = xs.shape[0]
    rim_x, rim_bc = from_behind((xs[steps_dev - width :], bc[steps_dev - width :]), "tm", 1)
    xa = causal_conv(xs, rim_x, conv_x)
    bca = causal_conv(bc, rim_bc, conv_bc)
    state_n = w_bc.shape[1] // 2
    bmat = bca[:, :state_n]
    cmat = bca[:, state_n:]
    dt = jax.nn.softplus(dt_raw + dt_bias)
    la = dt * -jnp.exp(a_log)
    heads = dt.shape[1]
    hdim = xa.shape[1] // heads
    blocks = steps_dev // BLOCK
    xa4 = xa.reshape(blocks, BLOCK, heads, hdim)
    b3 = bmat.reshape(blocks, BLOCK, state_n)
    c3 = cmat.reshape(blocks, BLOCK, state_n)
    dt3 = dt.reshape(blocks, BLOCK, heads)
    la3 = la.reshape(blocks, BLOCK, heads)
    ydiag, states, totals, cums = jax.vmap(block_terms)(xa4, b3, c3, dt3, la3)
    run_decay = jnp.ones((heads,), jnp.float32)
    run_state = jnp.zeros((heads, state_n, hdim), jnp.float32)
    before = []
    for index in range(blocks):
        before.append((run_decay, run_state))
        run_decay, run_state = combine_states(
            (run_decay, run_state), (totals[index], states[index])
        )
    identity = (jnp.ones_like(run_decay), jnp.zeros_like(run_state))
    _, incoming = prefix((run_decay, run_state), "tm", combine_states, identity)
    hins = jnp.stack([incoming * pair[0][:, None, None] + pair[1] for pair in before])
    ys = jax.vmap(block_output, in_axes=(0, 0, 0, 0, 0, None))(ydiag, cums, c3, hins, xa4, d_skip)
    y = ys.reshape(steps_dev, heads * hdim)
    gated = y * jax.nn.silu(gate.astype(jnp.float32))
    square = lax.psum(jnp.sum(gated * gated, axis=1), "head")
    inner = gated.shape[1] * lax.axis_size("head")
    yn = (gated * lax.rsqrt(square[:, None] / inner + 1e-05) * norm_gain).astype(jnp.bfloat16)
    mix_width = w_mix.shape[1]
    col_start = lax.axis_index("head") * mix_width
    share = steps_dev // lax.axis_size("head")
    row_start = lax.axis_index("head") * share
    summed = lax.psum_scatter(
        jnp.dot(yn, w_out, preferred_element_type=jnp.float32),
        "head",
        scatter_dimension=0,
        tiled=True,
    )
    hidden_rows = (lax.dynamic_slice_in_dim(u, row_start, share, 0) + summed).astype(jnp.bfloat16)
    piece = lax.all_gather(hidden_rows, "head", axis=0, tiled=True)
    own = lax.dynamic_slice_in_dim(piece, col_start, mix_width, 1).astype(jnp.float32)
    return (own + jnp.dot(piece, w_mix, preferred_element_type=jnp.float32)).astype(jnp.bfloat16)


def solution(mesh):
    in_specs = (
        P("tm", "head"),
        P(),
        P(),
        P(None, "head"),
        P(None, "head"),
        P(),
        P(None, "head"),
        P(None, "head"),
        P(),
        P("head"),
        P("head"),
        P("head"),
        P("head"),
        P("head", None),
        P(None, "head"),
    )
    out_specs = P("tm", "head")
    return jax.shard_map(shards, mesh=mesh, in_specs=in_specs, out_specs=out_specs, check_vma=False)
```

profile of v0, /device:TPU:2, one launch (start us, length us, event | category | flops | bytes accessed | tf_op | source)
XLA Modules:
  0.0 528.2 jit_solution(13383259743243343161)
XLA Ops:
  6.6 0.7 all-gather.5.cloned.1.call-update
  8.7 0.8 fusion.34
  9.5 0.9 fusion.33
  10.4 36.6 %all-gather.5.cloned.1.call-done = bf16[512,1024]{1,0:T(8,128)(2,1)} async-done(((bf16[512,256]{1,0:T(8,128)(2,1)}), bf16[512,1024]{1,0:T(8,128)(2,1)}) %all-gather.5.cloned.1.call-update) | async-done | bytes 1048592 | tf_op jit(solution)/shard_map/all_gather | solution.py:93
  47.0 2.9 convert_add_fusion
  50.4 1.2 reduce-window.6
  51.8 0.7 fusion.31
  52.7 1.6 convolution_convert_fusion.2
  54.3 1.9 collective-permute-start.1
  56.2 0.8 convolution_convert_fusion.1
  57.0 3.6 collective-permute-start
  60.6 0.7 collective-permute-done.1
  61.7 0.7 fusion.32
  62.3 0.7 convert_element_type.96
  63.1 1.0 collective-permute-done
  64.1 0.7 multiply_convert_fusion.12
  65.9 1.9 fusion.15
  67.8 0.8 slice_add_fusion
  69.4 76.6 %all-gather = f32[128,1,8]{2,1,0:T(1,128)S(1)} all-gather(f32[1,1,8]{2,1,0:T(1,128)S(1)} %get-tuple-element.98), channel_id=1, replica_groups=mesh['tm'=128,'head'=4] {'tm'}, dimensions={0}, use_global_device_ids=true | all-gather | bytes 4128 | tf_op jit(solution)/shard_map/all_gather | solution.py:18
  146.7 1.1 fusion.35
  147.7 114.8 %all-gather.7.cloned.1.call-done = f32[128,8,128,64]{2,3,1,0:T(8,128)} async-done(((f32[1,8,128,64]{2,3,1,0:T(8,128)}), f32[128,8,128,64]{2,3,1,0:T(8,128)}) %all-gather.7.cloned.1.call-update) | async-done | bytes 33554448 | tf_op jit(solution)/shard_map/all_gather | solution.py:18
  262.6 44.0 %while.12 = (s32[]{:T(128)}, f32[8,128,64]{2,1,0:T(8,128)S(1)}, s32[]{:T(128)}, f32[128,8]{1,0:T(8,128)S(1)}, f32[128,8,128,64]{2,3,1,0:T(8,128)}, /*index=5*/s32[]{:T(128)}, s32[]{:T(128)}, s32[]{:T(128)}) while((s32[]{:T(128)}, f32[8,128,64]{2,1,0:T(8,128)S(1)}, s32[]{:T(128)}, f32[128,8]{1,0:T(8,128)S(1)}, f32[128,8,128,64]{2,3,1,0:T(8,128)}, ...), condition=%wide.region_4.5_spmd, body=%wide.region_3.4_spmd.sunk | while | flops 131077 | bytes 1835231 | solution.py:26
  262.6 1.0 constant_dynamic-slice_fusion.2
  264.0 1.0 constant_dynamic-slice_fusion.2
  265.4 1.0 constant_dynamic-slice_fusion.2
  266.7 1.0 constant_dynamic-slice_fusion.2
  268.1 1.0 constant_dynamic-slice_fusion.2
  269.5 1.0 constant_dynamic-slice_fusion.2
  270.9 1.0 constant_dynamic-slice_fusion.2
  272.2 1.0 constant_dynamic-slice_fusion.2
  273.6 1.0 constant_dynamic-slice_fusion.2
  275.0 1.0 constant_dynamic-slice_fusion.2
  276.4 1.0 constant_dynamic-slice_fusion.2
  277.7 1.0 constant_dynamic-slice_fusion.2
  279.1 1.0 constant_dynamic-slice_fusion.2
  280.5 1.0 constant_dynamic-slice_fusion.2
  281.9 1.0 constant_dynamic-slice_fusion.2
  283.2 1.0 constant_dynamic-slice_fusion.2
  284.6 1.0 constant_dynamic-slice_fusion.2
  286.0 1.0 constant_dynamic-slice_fusion.2
  287.4 1.0 constant_dynamic-slice_fusion.2
  288.7 1.0 constant_dynamic-slice_fusion.2
  290.1 1.0 constant_dynamic-slice_fusion.2
  291.5 1.0 constant_dynamic-slice_fusion.2
  292.9 1.0 constant_dynamic-slice_fusion.2
  294.2 1.0 constant_dynamic-slice_fusion.2
  295.6 1.0 constant_dynamic-slice_fusion.2
  297.0 1.0 constant_dynamic-slice_fusion.2
  298.4 1.0 constant_dynamic-slice_fusion.2
  299.8 1.0 constant_dynamic-slice_fusion.2
  301.1 1.0 constant_dynamic-slice_fusion.2
  302.5 1.0 constant_dynamic-slice_fusion.2
  303.9 1.0 constant_dynamic-slice_fusion.2
  305.3 1.0 constant_dynamic-slice_fusion.2
  307.9 3.0 fusion.9
  310.9 2.0 copy.60
  312.9 1.5 reshape.92
  314.4 2.9 multiply_reduce_fusion.1
  317.2 10.5 %psum.7 = f32[512]{0:T(512)S(1)} all-reduce(f32[512]{0:T(512)S(1)} %get-tuple-element.101), channel_id=1, replica_groups=mesh['tm'=128,'head'=4] {'head'}, use_global_device_ids=true, to_apply=%region_6.7 | all-reduce | flops 512 | bytes 4096 | tf_op jit(solution)/shard_map/psum | solution.py:135
  327.7 2.1 fusion.20
  329.9 155.6 %reduce-scatter.2.cloned.1.call-done = f32[128,1024]{1,0:T(8,128)} async-done(((f32[512,1024]{1,0:T(8,128)}), f32[128,1024]{1,0:T(8,128)}) %reduce-scatter.2.cloned.1.call-update) | async-done | bytes 524304 | tf_op jit(solution)/shard_map/reduce_scatter | solution.py:142
  485.5 2.0 add_convert_fusion
  487.5 31.7 %all-gather.9.cloned.1.call-done = bf16[512,1024]{1,0:T(8,128)(2,1)} async-done(((bf16[128,1024]{1,0:T(8,128)(2,1)}), bf16[512,1024]{1,0:T(8,128)(2,1)}) %all-gather.9.cloned.1.call-update) | async-done | bytes 1048592 | tf_op jit(solution)/shard_map/all_gather | solution.py:149
  519.3 2.4 fusion.10
  (163 shorter events, 17.3 us)
Async XLA Ops:
  6.5 321.2 %copy-start = (bf16[512,1024]{1,0:T(8,128)(2,1)S(1)}, bf16[512,1024]{1,0:T(8,128)(2,1)}, u32[]{:S(2)}) copy-start(bf16[512,1024]{1,0:T(8,128)(2,1)} %param.30) | copy-start | bytes 3145732
  6.5 43.4 %copy-start.14 = (f32[1024]{0:T(1024)S(1)}, f32[1024]{0:T(1024)}, u32[]{:S(2)}) copy-start(f32[1024]{0:T(1024)} %param.19) | copy-start | bytes 12292
  6.5 43.4 %copy-start.13 = (bf16[1024,8]{0,1:T(8,128)(2,1)S(1)}, bf16[1024,8]{0,1:T(8,128)(2,1)}, u32[]{:S(2)}) copy-start(bf16[1024,8]{0,1:T(8,128)(2,1)} %param.23) | copy-start | bytes 49156
  6.5 43.4 %copy-start.16 = (f32[8]{0:T(128)S(1)}, f32[8]{0:T(128)}, u32[]{:S(2)}) copy-start(f32[8]{0:T(128)} %param.26) | copy-start | bytes 100
  6.5 40.5 %all-gather.5.cloned.1.call-start = ((), (), s32[]{:S(2)}) async-start(), calls=%async_computation.1 | async-start | bytes 1310720 | tf_op jit(solution)/shard_map/all_gather | solution.py:93
  7.3 255.3 %all-gather.7.cloned.1.call-start = ((), (), s32[]{:S(2)}) async-start(), calls=%async_computation.2 | async-start | bytes 33816576 | tf_op jit(solution)/shard_map/all_gather | solution.py:18
  47.0 2.9 copy-start.3
  50.4 6.6 %copy-start.6 = (f32[512,8]{0,1:T(8,128)}, f32[512,8]{0,1:T(8,128)S(1)}, u32[]{:S(2)}) copy-start(f32[512,8]{0,1:T(8,128)S(1)} %get-tuple-element.100) | copy-start | bytes 49156
  50.4 5.8 %copy-start.11 = (bf16[1024,512]{1,0:T(8,128)(2,1)S(1)}, bf16[1024,512]{1,0:T(8,128)(2,1)}, u32[]{:S(2)}) copy-start(bf16[1024,512]{1,0:T(8,128)(2,1)} %param.20) | copy-start | bytes 3145732
  54.3 7.0 %collective-permute-start.1 = (bf16[3,256]{1,0:T(4,128)(2,1)S(1)}, bf16[3,256]{1,0:T(4,128)(2,1)S(1)}, u32[]{:S(2)}, u32[]{:S(2)}) collective-permute-start(bf16[3,256]{1,0:T(4,128)(2,1)S(1)} %slice.106), channel_id=1, source_target_pairs={{0,4},{4,8},{8,12},{12,16},{16,20},{20,24},{24,28},{28,32},{32,36}... | collective-permute-start | bytes 4616 | tf_op jit(solution)/shard_map/ppermute | solution.py:13
  57.0 7.0 %collective-permute-start = (bf16[3,512]{1,0:T(4,128)(2,1)S(1)}, bf16[3,512]{1,0:T(4,128)(2,1)S(1)}, u32[]{:S(2)}, u32[]{:S(2)}) collective-permute-start(bf16[3,512]{1,0:T(4,128)(2,1)S(1)} %slice.101), channel_id=1, source_target_pairs={{0,4},{4,8},{8,12},{12,16},{16,20},{20,24},{24,28},{28,32},{32,36}... | collective-permute-start | bytes 9224 | tf_op jit(solution)/shard_map/ppermute | solution.py:13
  65.3 81.4 %copy-start.1 = (bf16[512,128]{1,0:T(8,128)(2,1)S(1)}, bf16[512,128]{1,0:T(8,128)(2,1)}, u32[]{:S(2)}) copy-start(bf16[512,128]{1,0:T(8,128)(2,1)} %get-tuple-element.87) | copy-start | bytes 393220
  68.7 416.9 %reduce-scatter.2.cloned.1.call-start = ((), (), s32[]{:S(2)}) async-start(), calls=%async_computation.3 | async-start | bytes 2621440 | tf_op jit(solution)/shard_map/reduce_scatter | solution.py:142
  306.6 0.9 copy-start.2
  306.6 1.2 copy-start.4
  306.8 1.0 copy-start.5
  306.8 1.0 copy-start.7
  306.8 1.0 copy-start.8
  306.9 1.0 copy-start.9
  312.9 1.5 copy-start.15
  314.4 13.4 %copy-start.10 = (f32[512]{0:T(512)S(1)}, f32[512]{0:T(512)}, u32[]{:S(2)}) copy-start(f32[512]{0:T(512)} %param.29) | copy-start | bytes 6148
  329.9 189.4 %copy-start.12 = (bf16[1024,256]{1,0:T(8,128)(2,1)S(1)}, bf16[1024,256]{1,0:T(8,128)(2,1)}, u32[]{:S(2)}) copy-start(bf16[1024,256]{1,0:T(8,128)(2,1)} %param.31) | copy-start | bytes 1572868
  329.9 189.4 %all-gather.9.cloned.1.call-start = ((), (), s32[]{:S(2)}) async-start(), calls=%async_computation.4 | async-start | bytes 1310720 | tf_op jit(solution)/shard_map/all_gather | solution.py:149
Sparse Core Ops, SparseCore 0:
  9.4 37.5 all-gather.4
  68.8 193.7 all-gather.6
  330.0 155.4 reduce-scatter.1
  487.6 31.5 all-gather.8
where the time goes:
time: 533 us; the launch traced here: 528 us
  waiting for transfers between devices  341 us (64%)
  blocking collectives  87.1 us (16%)
  local copies, waits for them, and re-layouts  46 us (9%)
  matrix products  16.5 us (3%)
  other arithmetic  16.1 us (3%)
  between operations  14.1 us (3%)
  starting transfers between devices  5.65 us (1%)
    reduce_scatter x1, waiting for transfers between devices, shards(): lax.psum_scatter(jnp.dot(yn, w_out, preferred_element_type=jnp.float32),...  156 us
    all_gather x1, waiting for transfers between devices, prefix(): gathered = jax.tree.map(lambda a: lax.all_gather(a, axis), part)  115 us
    all_gather x1, blocking collectives, prefix(): gathered = jax.tree.map(lambda a: lax.all_gather(a, axis), part)  76.6 us
    dynamic_slice x64, local copies, waits for them, and re-layouts, one(): lax.dynamic_index_in_dim(a, hop, 0, False)  37.5 us
    all_gather x1, waiting for transfers between devices, shards(): whole = lax.all_gather(latent, 'head', axis=1, tiled=True)  36.6 us
    all_gather x1, waiting for transfers between devices, shards(): piece = lax.all_gather(hidden_rows, 'head', axis=0, tiled=True)  31.7 us
  transfers between devices with their start and end apart: 6, of which 6 were waited for; matrix products, arithmetic and copies ran while one was open for 1% of the time, Pallas kernels for 0%

commit v1 on v0

--- a/solution.py
+++ b/solution.py
@@ -90,7 +90,24 @@
     w_out,
     w_mix,
 ):
-    whole = lax.all_gather(latent, "head", axis=1, tiled=True)
+    block_next = lax.axis_size("head")
+    mixed_arr, step_out, oldest = (block_next, lax.axis_index("head"), latent.shape[1])
+    views = [(d, (d + 1) % mixed_arr) for d in range(mixed_arr)]
+    trail = [(d, (d - 1) % mixed_arr) for d in range(mixed_arr)]
+    whole = jnp.zeros((*latent.shape[:1], mixed_arr * oldest, *latent.shape[2:]), latent.dtype)
+    whole = lax.dynamic_update_slice_in_dim(whole, latent, step_out * oldest, axis=1)
+    value_now = z1 = latent
+    f_next = mixed_arr // 2
+    for tick in range(1, f_next + 1):
+        value_now = lax.ppermute(value_now, "head", views)
+        whole = lax.dynamic_update_slice_in_dim(
+            whole, value_now, (step_out - tick) % mixed_arr * oldest, axis=1
+        )
+        if tick < mixed_arr - f_next:
+            z1 = lax.ppermute(z1, "head", trail)
+            whole = lax.dynamic_update_slice_in_dim(
+                whole, z1, (step_out + tick) % mixed_arr * oldest, axis=1
+            )
     u = whole.astype(jnp.float32) + sinusoid(timestep, whole.shape[1])[None, :]
     normed = (u * lax.rsqrt(jnp.mean(u * u, axis=1, keepdims=True) + 1e-05) * in_gain).astype(
         jnp.bfloat16

time: 533 us -> 514 us (0.964)
  waiting for transfers between devices: 341 us -> 313 us
  starting transfers between devices: 5.65 us -> 15.3 us
    all_gather x1 -> x0, waiting for transfers between devices: 36.6 us -> none  [shards(): whole = lax.all_gather(latent, 'head', axis=1, tiled=True)]
    ppermute x0 -> x3, starting transfers between devices: none -> 9.37 us  [the longest x2 5.8 us: shards(): value_now = lax.ppermute(value_now, 'head', views)]
    ppermute x0 -> x3, waiting for transfers between devices: none -> 8.28 us  [the longest x2 8.28 us: shards(): value_now = lax.ppermute(value_now, 'head', views)]
  transfers between devices with their start and end apart: 6 -> 8, of which waited for: 6 -> 7; matrix products, arithmetic and copies ran while one was open for 1% -> 2% of each run, Pallas kernels for 0% -> 0%
where the time goes in v1:
time: 514 us; the launch traced here: 510 us
  waiting for transfers between devices  313 us (61%)
  blocking collectives  86.4 us (17%)
  local copies, waits for them, and re-layouts  47.2 us (9%)
  matrix products  16.5 us (3%)
  starting transfers between devices  15.3 us (3%)
  other arithmetic  14.9 us (3%)
  between operations  14.3 us (3%)
    reduce_scatter x1, waiting for transfers between devices, shards(): lax.psum_scatter(jnp.dot(yn, w_out, preferred_element_type=jnp.float32),...  156 us
    all_gather x1, waiting for transfers between devices, prefix(): gathered = jax.tree.map(lambda a: lax.all_gather(a, axis), part)  113 us
    all_gather x1, blocking collectives, prefix(): gathered = jax.tree.map(lambda a: lax.all_gather(a, axis), part)  76 us
    dynamic_slice x64, local copies, waits for them, and re-layouts, one(): lax.dynamic_index_in_dim(a, hop, 0, False)  37.5 us
    all_gather x1, waiting for transfers between devices, shards(): piece = lax.all_gather(hidden_rows, 'head', axis=0, tiled=True)  31.8 us
    psum x1, blocking collectives, shards(): square = lax.psum(jnp.sum(gated * gated, axis=1), 'head')  10.5 us
  transfers between devices with their start and end apart: 8, of which 7 were waited for; matrix products, arithmetic and copies ran while one was open for 2% of the time, Pallas kernels for 0%

profile of v1, /device:TPU:2, one launch (start us, length us, event | category | flops | bytes accessed | tf_op | source)
XLA Modules:
  0.0 509.5 jit_solution(8961709530280016243)
XLA Ops:
  6.5 3.6 collective-permute-start
  10.2 3.6 collective-permute-start.1
  13.7 0.8 fusion.34
  14.6 0.9 fusion.33
  16.9 1.0 constant_dynamic-update-slice_fusion.3
  18.1 2.2 collective-permute-start.2
  20.5 8.1 %collective-permute-done.2 = bf16[512,256]{1,0:T(8,128)(2,1)S(1)} collective-permute-done((bf16[512,256]{1,0:T(8,128)(2,1)S(1)}, bf16[512,256]{1,0:T(8,128)(2,1)S(1)}, u32[]{:S(2)}, u32[]{:S(2)}) %collective-permute-start.2) | collective-permute-done | bytes 262176 | tf_op jit(solution)/shard_map/ppermute | solution.py:102
  28.6 1.6 convert_add_fusion
  30.8 1.2 reduce-window.6
  33.1 1.5 convolution_convert_fusion.2
  34.6 1.9 collective-permute-start.4
  36.6 0.8 convolution_convert_fusion.1
  37.4 3.9 collective-permute-start.3
  41.4 3.9 collective-permute-done.4
  46.3 0.7 convert_element_type.96
  47.0 1.0 collective-permute-done.3
  49.8 1.9 fusion.15
  51.8 0.8 slice_add_fusion
  53.3 76.0 %all-gather = f32[128,1,8]{2,1,0:T(1,128)S(1)} all-gather(f32[1,1,8]{2,1,0:T(1,128)S(1)} %get-tuple-element.98), channel_id=1, replica_groups=mesh['tm'=128,'head'=4] {'tm'}, dimensions={0}, use_global_device_ids=true | all-gather | bytes 4128 | tf_op jit(solution)/shard_map/all_gather | solution.py:18
  130.0 1.1 fusion.35
  131.0 112.8 %all-gather.4.cloned.1.call-done = f32[128,8,128,64]{2,3,1,0:T(8,128)} async-done(((f32[1,8,128,64]{2,3,1,0:T(8,128)}), f32[128,8,128,64]{2,3,1,0:T(8,128)}) %all-gather.4.cloned.1.call-update) | async-done | bytes 33554448 | tf_op jit(solution)/shard_map/all_gather | solution.py:18
  243.9 44.0 %while.12 = (s32[]{:T(128)}, f32[8,128,64]{2,1,0:T(8,128)S(1)}, s32[]{:T(128)}, f32[128,8]{1,0:T(8,128)S(1)}, f32[128,8,128,64]{2,3,1,0:T(8,128)}, /*index=5*/s32[]{:T(128)}, s32[]{:T(128)}, s32[]{:T(128)}) while((s32[]{:T(128)}, f32[8,128,64]{2,1,0:T(8,128)S(1)}, s32[]{:T(128)}, f32[128,8]{1,0:T(8,128)S(1)}, f32[128,8,128,64]{2,3,1,0:T(8,128)}, ...), condition=%wide.region_4.5_spmd, body=%wide.region_3.4_spmd.sunk | while | flops 131077 | bytes 1835231 | solution.py:26
  243.9 1.0 constant_dynamic-slice_fusion.2
  245.3 1.0 constant_dynamic-slice_fusion.2
  246.7 1.0 constant_dynamic-slice_fusion.2
  248.0 1.0 constant_dynamic-slice_fusion.2
  249.4 1.0 constant_dynamic-slice_fusion.2
  250.8 1.0 constant_dynamic-slice_fusion.2
  252.2 1.0 constant_dynamic-slice_fusion.2
  253.5 1.0 constant_dynamic-slice_fusion.2
  254.9 1.0 constant_dynamic-slice_fusion.2
  256.3 1.0 constant_dynamic-slice_fusion.2
  257.7 1.0 constant_dynamic-slice_fusion.2
  259.0 1.0 constant_dynamic-slice_fusion.2
  260.4 1.0 constant_dynamic-slice_fusion.2
  261.8 1.0 constant_dynamic-slice_fusion.2
  263.2 1.0 constant_dynamic-slice_fusion.2
  264.6 1.0 constant_dynamic-slice_fusion.2
  265.9 1.0 constant_dynamic-slice_fusion.2
  267.3 1.0 constant_dynamic-slice_fusion.2
  268.7 1.0 constant_dynamic-slice_fusion.2
  270.1 1.0 constant_dynamic-slice_fusion.2
  271.4 1.0 constant_dynamic-slice_fusion.2
  272.8 1.0 constant_dynamic-slice_fusion.2
  274.2 1.0 constant_dynamic-slice_fusion.2
  275.6 1.0 constant_dynamic-slice_fusion.2
  276.9 1.0 constant_dynamic-slice_fusion.2
  278.3 1.0 constant_dynamic-slice_fusion.2
  279.7 1.0 constant_dynamic-slice_fusion.2
  281.1 1.0 constant_dynamic-slice_fusion.2
  282.4 1.0 constant_dynamic-slice_fusion.2
  283.8 1.0 constant_dynamic-slice_fusion.2
  285.2 1.0 constant_dynamic-slice_fusion.2
  286.6 1.0 constant_dynamic-slice_fusion.2
  289.2 3.0 fusion.9
  292.2 2.0 copy.60
  294.2 1.5 reshape.92
  295.7 2.9 multiply_reduce_fusion.1
  298.6 10.5 %psum.7 = f32[512]{0:T(512)S(1)} all-reduce(f32[512]{0:T(512)S(1)} %get-tuple-element.101), channel_id=1, replica_groups=mesh['tm'=128,'head'=4] {'head'}, use_global_device_ids=true, to_apply=%region_6.7 | all-reduce | flops 512 | bytes 4096 | tf_op jit(solution)/shard_map/psum | solution.py:152
  309.1 2.1 fusion.20
  311.2 155.6 %reduce-scatter.2.cloned.1.call-done = f32[128,1024]{1,0:T(8,128)} async-done(((f32[512,1024]{1,0:T(8,128)}), f32[128,1024]{1,0:T(8,128)}) %reduce-scatter.2.cloned.1.call-update) | async-done | bytes 524304 | tf_op jit(solution)/shard_map/reduce_scatter | solution.py:159
  466.8 2.0 add_convert_fusion
  468.8 31.8 %all-gather.6.cloned.1.call-done = bf16[512,1024]{1,0:T(8,128)(2,1)} async-done(((bf16[128,1024]{1,0:T(8,128)(2,1)}), bf16[512,1024]{1,0:T(8,128)(2,1)}) %all-gather.6.cloned.1.call-update) | async-done | bytes 1048592 | tf_op jit(solution)/shard_map/all_gather | solution.py:166
  500.6 2.4 fusion.10
  (171 shorter events, 19.7 us)
Async XLA Ops:
  6.5 302.5 %copy-start = (bf16[512,1024]{1,0:T(8,128)(2,1)S(1)}, bf16[512,1024]{1,0:T(8,128)(2,1)}, u32[]{:S(2)}) copy-start(bf16[512,1024]{1,0:T(8,128)(2,1)} %param.30) | copy-start | bytes 3145732
  6.5 237.3 %all-gather.4.cloned.1.call-start = ((), (), s32[]{:S(2)}) async-start(), calls=%async_computation.1 | async-start | bytes 33816576 | tf_op jit(solution)/shard_map/all_gather | solution.py:18
  6.5 11.6 %collective-permute-start = (bf16[512,256]{1,0:T(8,128)(2,1)}, bf16[512,256]{1,0:T(8,128)(2,1)S(1)}, u32[]{:S(2)}, u32[]{:S(2)}) collective-permute-start(bf16[512,256]{1,0:T(8,128)(2,1)} %param.17), channel_id=1, source_target_pairs={{0,1},{1,2},{2,3},{3,0},{4,5},{5,6},{6,7},{7,4},{8,9},{9,10},{10,1... | collective-permute-start | bytes 786440 | tf_op jit(solution)/shard_map/ppermute | solution.py:102
  10.2 10.3 %collective-permute-start.1 = (bf16[512,256]{1,0:T(8,128)(2,1)}, bf16[512,256]{1,0:T(8,128)(2,1)S(1)}, u32[]{:S(2)}, u32[]{:S(2)}) collective-permute-start(bf16[512,256]{1,0:T(8,128)(2,1)} %param.17), channel_id=1, source_target_pairs={{0,3},{1,0},{2,1},{3,2},{4,7},{5,4},{6,5},{7,6},{8,11},{9,8},{10,9... | collective-permute-start | bytes 786440 | tf_op jit(solution)/shard_map/ppermute | solution.py:107
  18.1 10.5 %collective-permute-start.2 = (bf16[512,256]{1,0:T(8,128)(2,1)S(1)}, bf16[512,256]{1,0:T(8,128)(2,1)S(1)}, u32[]{:S(2)}, u32[]{:S(2)}) collective-permute-start(bf16[512,256]{1,0:T(8,128)(2,1)S(1)} %collective-permute-done), channel_id=1, source_target_pairs={{0,1},{1,2},{2,3},{3,0},{4,5},{5,6},{6,7},{7,4},{8,9},{9,10},{10,1... | collective-permute-start | bytes 786440 | tf_op jit(solution)/shard_map/ppermute | solution.py:102
  20.4 9.9 %copy-start.13 = (bf16[1024,8]{0,1:T(8,128)(2,1)S(1)}, bf16[1024,8]{0,1:T(8,128)(2,1)}, u32[]{:S(2)}) copy-start(bf16[1024,8]{0,1:T(8,128)(2,1)} %param.23) | copy-start | bytes 49156
  20.4 9.9 %copy-start.14 = (f32[1024]{0:T(1024)S(1)}, f32[1024]{0:T(1024)}, u32[]{:S(2)}) copy-start(f32[1024]{0:T(1024)} %param.19) | copy-start | bytes 12292
  20.4 9.9 %copy-start.16 = (f32[8]{0:T(128)S(1)}, f32[8]{0:T(128)}, u32[]{:S(2)}) copy-start(f32[8]{0:T(128)} %param.26) | copy-start | bytes 100
  28.6 8.0 %copy-start.1 = (bf16[512,1024]{1,0:T(8,128)(2,1)}, bf16[512,1024]{1,0:T(8,128)(2,1)S(1)}, u32[]{:S(2)}) copy-start(bf16[512,1024]{1,0:T(8,128)(2,1)S(1)} %constant_dynamic-update-slice_fusion) | copy-start | bytes 3145732
  30.8 6.6 %copy-start.6 = (f32[512,8]{0,1:T(8,128)}, f32[512,8]{0,1:T(8,128)S(1)}, u32[]{:S(2)}) copy-start(f32[512,8]{0,1:T(8,128)S(1)} %get-tuple-element.100) | copy-start | bytes 49156
  30.8 5.8 %copy-start.11 = (bf16[1024,512]{1,0:T(8,128)(2,1)S(1)}, bf16[1024,512]{1,0:T(8,128)(2,1)}, u32[]{:S(2)}) copy-start(bf16[1024,512]{1,0:T(8,128)(2,1)} %param.20) | copy-start | bytes 3145732
  34.6 10.6 %collective-permute-start.4 = (bf16[3,256]{1,0:T(4,128)(2,1)S(1)}, bf16[3,256]{1,0:T(4,128)(2,1)S(1)}, u32[]{:S(2)}, u32[]{:S(2)}) collective-permute-start(bf16[3,256]{1,0:T(4,128)(2,1)S(1)} %slice.106), channel_id=1, source_target_pairs={{0,4},{4,8},{8,12},{12,16},{16,20},{20,24},{24,28},{28,32},{32,36}... | collective-permute-start | bytes 4616 | tf_op jit(solution)/shard_map/ppermute | solution.py:13
  37.4 10.6 %collective-permute-start.3 = (bf16[3,512]{1,0:T(4,128)(2,1)S(1)}, bf16[3,512]{1,0:T(4,128)(2,1)S(1)}, u32[]{:S(2)}, u32[]{:S(2)}) collective-permute-start(bf16[3,512]{1,0:T(4,128)(2,1)S(1)} %slice.101), channel_id=1, source_target_pairs={{0,4},{4,8},{8,12},{12,16},{16,20},{20,24},{24,28},{28,32},{32,36}... | collective-permute-start | bytes 9224 | tf_op jit(solution)/shard_map/ppermute | solution.py:13
  49.2 80.7 %copy-start.2 = (bf16[512,128]{1,0:T(8,128)(2,1)S(1)}, bf16[512,128]{1,0:T(8,128)(2,1)}, u32[]{:S(2)}) copy-start(bf16[512,128]{1,0:T(8,128)(2,1)} %get-tuple-element.87) | copy-start | bytes 393220
  52.6 414.2 %reduce-scatter.2.cloned.1.call-start = ((), (), s32[]{:S(2)}) async-start(), calls=%async_computation.2 | async-start | bytes 2621440 | tf_op jit(solution)/shard_map/reduce_scatter | solution.py:159
  287.9 0.9 copy-start.3
  287.9 1.2 copy-start.4
  288.1 1.0 copy-start.5
  288.1 1.0 copy-start.7
  288.2 1.0 copy-start.8
  288.2 1.0 copy-start.9
  294.2 1.5 copy-start.15
  295.7 13.4 %copy-start.10 = (f32[512]{0:T(512)S(1)}, f32[512]{0:T(512)}, u32[]{:S(2)}) copy-start(f32[512]{0:T(512)} %param.29) | copy-start | bytes 6148
  311.2 189.4 %copy-start.12 = (bf16[1024,256]{1,0:T(8,128)(2,1)S(1)}, bf16[1024,256]{1,0:T(8,128)(2,1)}, u32[]{:S(2)}) copy-start(bf16[1024,256]{1,0:T(8,128)(2,1)} %param.31) | copy-start | bytes 1572868
  311.2 189.4 %all-gather.6.cloned.1.call-start = ((), (), s32[]{:S(2)}) async-start(), calls=%async_computation.3 | async-start | bytes 1310720 | tf_op jit(solution)/shard_map/all_gather | solution.py:166
Sparse Core Ops, SparseCore 0:
  52.7 191.0 all-gather.3
  311.3 155.4 reduce-scatter.1
  468.9 31.5 all-gather.5
